TPU v7x, 128 devices: a whole 4x4x4 slice. The times are simulated.
128 devices in a mesh: group: 32 (over z, y, x_hi), head: 4 (over x_lo, core).
Axes of the slice: x: 4 (x_hi: 2, x_lo: 2; x = x_hi * 2 + x_lo), y: 4, z: 4, core: 2. Of those that a mesh axis runs over, the one named last changes fastest.
Arguments:
- tokens: bfloat16 [4, 4096, 1536], P(None, 'group'), may hold values from -6 to 6
- parents: int32 [3, 4096], P(None, 'group'), may hold values from 0 to 7
- page_request: int32 [1536], P('group'), may hold values from 0 to 511, as said below
- page_fill: int32 [1536], P('group'), may hold values from 1 to 128, as said below
- keys_pool: bfloat16 [1536, 1536, 128], P('group', 'head'), may hold values from -600 to 600
- values_pool: bfloat16 [1536, 1536, 128], P('group', 'head'), may hold values from -6 to 6
- decay_pool: bfloat16 [1536, 24, 128], P('group', 'head'), may hold values from -494.52 to 0
- gain_attn: float32 [1536], replicated, may hold values from 0.1 to 1.9
- w_query: bfloat16 [1536, 1536], P('head'), may hold values from -0.15625 to 0.15625
- w_key: bfloat16 [1536, 1536], P('head'), may hold values from -0.15625 to 0.15625
- w_value: bfloat16 [1536, 1536], P('head'), may hold values from -0.15625 to 0.15625
- w_forget: bfloat16 [1536, 24], P(None, 'head'), may hold values from -0.15625 to 0.15625
- forget_bias: float32 [24], P('head'), may hold values from -2 to 6
- w_out: bfloat16 [1536, 1536], P('head'), may hold values from -0.15625 to 0.15625
- gain_ffn: float32 [1536], replicated, may hold values from 0.1 to 1.9
- w_gate: bfloat16 [1536, 4096], P(None, 'head'), may hold values from -0.15625 to 0.15625
- w_up: bfloat16 [1536, 4096], P(None, 'head'), may hold values from -0.15625 to 0.15625
- w_down: bfloat16 [4096, 1536], P('head'), may hold values from -0.09375 to 0.09375
Outputs:
- outputs: bfloat16 [4, 4096, 1536], P(None, 'group')
Inputs may be any that keep to these rules, and one draw needn't show every extreme that they name: `page_request`: request ids g * 16 to g * 16 + 15 are the requests owned by group g, and pages g * 48 to g * 48 + 47 are the page slots of group g. The first 32 slots of a group hold pages of its own requests; its other 16 slots hold pages of other groups' requests, at most 1 from the requests of one group. Every request has at least one page. `page_fill`: the valid positions of a page are its first ones.
All inputs are finite; a program needn't handle non-finite values.
Results may differ from a plain program's by a relative error of at most 0.0095.
Values may be sent and summed in bfloat16 or wider, within the bound.
A program may use at most 192 MiB of HBM per device.

v0:
```python
import jax
import jax.numpy as jnp
from jax import lax
from jax.sharding import PartitionSpec as P

BEAMS = 8
OWNED_SLOTS = 32
SPILL = 16
epsilon = 1e-05
masked_score = -1e30


def rms_scale(values, gain_vector):
    widened = values.astype(jnp.float32)
    return (
        widened
        * lax.rsqrt(jnp.mean(widened * widened, axis=-1, keepdims=True) + epsilon)
        * gain_vector
    )


def page_partials(page_keys, page_values, page_decay, fill_count, asked_rows, head_count):
    page_count, inner_width, length = page_keys.shape
    head_size = inner_width // head_count
    keys_split = page_keys.reshape(page_count, head_count, head_size, length)
    values_split = page_values.reshape(page_count, head_count, head_size, length)
    asked_split = asked_rows.reshape(asked_rows.shape[:3] + (head_count, head_size))
    scores = jnp.einsum(
        "pbshd,phdt->pbsht", asked_split, keys_split, preferred_element_type=jnp.float32
    ) * head_size ** (-0.5)
    scores = scores + page_decay.astype(jnp.float32)[:, None, None, :, :]
    valid_mask = jnp.arange(length)[None, :] < fill_count[:, None]
    scores = jnp.where(valid_mask[:, None, None, None, :], scores, masked_score)
    page_top = jnp.max(scores, axis=-1)
    weights = jnp.exp(scores - page_top[..., None])
    page_total = jnp.sum(weights, axis=-1)
    numerator = jnp.einsum(
        "pbsht,phdt->pbshd",
        weights.astype(jnp.bfloat16),
        values_split,
        preferred_element_type=jnp.float32,
    )
    return (page_top, page_total, numerator.reshape(numerator.shape[:3] + (inner_width,)))


def by_request(current_request, page_top, page_total, numerator, request_count, head_count):
    matches = current_request[None, :] == jnp.arange(request_count)[:, None]
    wide_match = matches[:, :, None, None, None]
    best_top = jnp.max(jnp.where(wide_match, page_top[None], masked_score), axis=1)
    factor = jnp.where(wide_match, jnp.exp(page_top[None] - best_top[:, None]), 0.0)
    summed = jnp.sum(factor * page_total[None], axis=1)
    numer_split = numerator.reshape(numerator.shape[:3] + (head_count, -1))
    combined = jnp.sum(factor[..., None] * numer_split[None], axis=1)
    return (best_top, summed, combined.reshape(combined.shape[:3] + (-1,)))


def shards(
    tokens,
    parents,
    page_request,
    page_fill,
    keys_pool,
    values_pool,
    decay_pool,
    gain_attn,
    w_query,
    w_key,
    w_value,
    w_forget,
    forget_bias,
    w_out,
    gain_ffn,
    w_gate,
    w_up,
    w_down,
):
    step_count, row_count, model_width = tokens.shape
    head_count = w_forget.shape[1]
    inner_width = w_query.shape[0]
    head_size = inner_width // head_count
    local_count = row_count // BEAMS
    groups = lax.axis_size("group")
    own_group = lax.axis_index("group")
    capacity = (SPILL + groups - 2) // (groups - 1)
    flat_tokens = tokens.reshape(step_count * row_count, model_width)
    normed = rms_scale(flat_tokens, gain_attn).astype(jnp.bfloat16)

    def project(weight):
        product = lax.dot_general(
            normed, weight, (((1,), (1,)), ((), ())), preferred_element_type=jnp.float32
        )
        return product.astype(jnp.bfloat16).reshape(step_count, row_count, -1)

    queries = project(w_query)
    key_new = project(w_key)
    value_new = project(w_value)
    forget = jax.nn.log_sigmoid(
        jnp.dot(normed, w_forget, preferred_element_type=jnp.float32) + forget_bias
    ).reshape(step_count, row_count, head_count)
    by_row = queries.transpose(1, 0, 2)
    by_request_rows = by_row.reshape(local_count, BEAMS, step_count, inner_width)
    own_request = page_request[:OWNED_SLOTS] - own_group * local_count
    own_parts = page_partials(
        keys_pool[:OWNED_SLOTS],
        values_pool[:OWNED_SLOTS],
        decay_pool[:OWNED_SLOTS],
        page_fill[:OWNED_SLOTS],
        by_request_rows[own_request],
        head_count,
    )
    hosted_request = page_request[OWNED_SLOTS:]
    hosted_owner = hosted_request // local_count
    hosted_local = hosted_request % local_count
    hosted_index = jnp.arange(hosted_request.shape[0])
    earlier = (hosted_owner[:, None] == hosted_owner[None, :]) & (
        hosted_index[None, :] < hosted_index[:, None]
    )
    hosted_rank = jnp.sum(earlier, axis=1)
    slot_match = (hosted_owner[None, None, :] == jnp.arange(groups)[:, None, None]) & (
        hosted_rank[None, None, :] == jnp.arange(capacity)[None, :, None]
    )
    slot_full = jnp.any(slot_match, axis=2)
    slot_source = jnp.sum(jnp.where(slot_match, hosted_index[None, None, :], 0), axis=2)
    slot_local = jnp.sum(jnp.where(slot_match, hosted_local[None, None, :], 0), axis=2)
    slot_count = groups * capacity
    base_rows = jnp.arange(row_count) // BEAMS * BEAMS
    hist_keys = jnp.zeros((0, row_count, inner_width), jnp.bfloat16)
    hist_values = jnp.zeros((0, row_count, inner_width), jnp.bfloat16)
    hist_totals = jnp.zeros((0, row_count, head_count), jnp.float32)
    running = jnp.zeros((row_count, head_count), jnp.float32)
    finished = []
    for step_index in range(step_count):
        query_block = by_row[:, step_index : step_index + 1]
        step_span = query_block.shape[1]
        gathered = lax.all_gather(query_block, "group", axis=0, tiled=True)
        asked_rows = gathered.reshape(groups * local_count, BEAMS, step_span, inner_width)[
            hosted_request
        ]
        page_top, page_total, numerator = page_partials(
            keys_pool[OWNED_SLOTS:],
            values_pool[OWNED_SLOTS:],
            decay_pool[OWNED_SLOTS:],
            page_fill[OWNED_SLOTS:],
            asked_rows,
            head_count,
        )
        full_slot = slot_full[:, :, None, None, None]
        own_now = tuple((member[:, :, step_index : step_index + 1] for member in own_parts))
        all_request = jnp.concatenate(
            [
                own_request,
                lax.all_to_all(
                    slot_local.astype(jnp.float32), "group", split_axis=0, concat_axis=0, tiled=True
                )
                .reshape(slot_count)
                .astype(jnp.int32),
            ],
            axis=0,
        )
        all_top = jnp.concatenate(
            [
                own_now[0],
                lax.all_to_all(
                    jnp.where(full_slot, page_top[slot_source], masked_score),
                    "group",
                    split_axis=0,
                    concat_axis=0,
                    tiled=True,
                ).reshape((slot_count,) + page_top.shape[1:]),
            ],
            axis=0,
        )
        all_total = jnp.concatenate(
            [
                own_now[1],
                lax.all_to_all(
                    jnp.where(full_slot, page_total[slot_source], 0.0),
                    "group",
                    split_axis=0,
                    concat_axis=0,
                    tiled=True,
                ).reshape((slot_count,) + page_total.shape[1:]),
            ],
            axis=0,
        )
        all_numer = jnp.concatenate(
            [
                own_now[2],
                lax.all_to_all(
                    jnp.where(full_slot, numerator[slot_source], 0.0),
                    "group",
                    split_axis=0,
                    concat_axis=0,
                    tiled=True,
                ).reshape((slot_count,) + numerator.shape[1:]),
            ],
            axis=0,
        )
        page_top, page_total, page_numer = by_request(
            all_request, all_top, all_total, all_numer, local_count, head_count
        )
        page_top = page_top.reshape(row_count, head_count)
        page_total = page_total.reshape(row_count, head_count)
        page_numer = page_numer.reshape(row_count, head_count, head_size)
        if step_index > 0:
            source = base_rows + parents[step_index - 1]
            hist_keys = hist_keys[:, source]
            hist_values = hist_values[:, source]
            hist_totals = hist_totals[:, source]
            running = running[source]
        running = running + forget[step_index]
        hist_keys = jnp.concatenate([hist_keys, key_new[step_index][None]], axis=0)
        hist_values = jnp.concatenate([hist_values, value_new[step_index][None]], axis=0)
        hist_totals = jnp.concatenate([hist_totals, running[None]], axis=0)
        asked_now = queries[step_index].reshape(row_count, head_count, head_size)
        keys_now = hist_keys.reshape(step_index + 1, row_count, head_count, head_size)
        values_now = hist_values.reshape(step_index + 1, row_count, head_count, head_size)
        scores = jnp.einsum(
            "rhd,urhd->rhu", asked_now, keys_now, preferred_element_type=jnp.float32
        ) * head_size ** (-0.5) - hist_totals.transpose(1, 2, 0)
        history_top = jnp.max(scores, axis=-1)
        weights = jnp.exp(scores - history_top[..., None])
        history_total = jnp.sum(weights, axis=-1)
        history_numer = jnp.einsum(
            "rhu,urhd->rhd",
            weights.astype(jnp.bfloat16),
            values_now,
            preferred_element_type=jnp.float32,
        )
        best_top = jnp.maximum(page_top, history_top)
        page_scale = jnp.exp(page_top - best_top)
        history_scale = jnp.exp(history_top - best_top)
        total_sum = page_total * page_scale + history_total * history_scale
        numer_sum = page_numer * page_scale[..., None] + history_numer * history_scale[..., None]
        attended = (
            (numer_sum / total_sum[..., None]).astype(jnp.bfloat16).reshape(row_count, inner_width)
        )
        mixed_sum = lax.psum(jnp.dot(attended, w_out, preferred_element_type=jnp.float32), "head")
        residual = tokens[step_index].astype(jnp.float32) + mixed_sum
        normed_ffn = rms_scale(residual, gain_ffn).astype(jnp.bfloat16)
        gate_proj = jnp.dot(normed_ffn, w_gate, preferred_element_type=jnp.float32)
        up_proj = jnp.dot(normed_ffn, w_up, preferred_element_type=jnp.float32)
        hidden = (jax.nn.silu(gate_proj) * up_proj).astype(jnp.bfloat16)
        down_sum = lax.psum(jnp.dot(hidden, w_down, preferred_element_type=jnp.float32), "head")
        finished.append((residual + down_sum).astype(jnp.bfloat16))
    result = jnp.stack(finished, axis=0)
    return result


def solution(mesh):
    return jax.shard_map(
        shards,
        mesh=mesh,
        in_specs=(
            P(None, "group", None),
            P(None, "group"),
            P("group"),
            P("group"),
            P("group", "head", None),
            P("group", "head", None),
            P("group", "head", None),
            P(),
            P("head", None),
            P("head", None),
            P("head", None),
            P(None, "head"),
            P("head"),
            P("head", None),
            P(),
            P(None, "head"),
            P(None, "head"),
            P("head", None),
        ),
        out_specs=P(None, "group", None),
        check_vma=False,
    )
```

profile of v0, /device:TPU:1, one launch (start us, length us, event | category | flops | bytes accessed | tf_op | source)
XLA Modules:
  0.0 839.9 jit_solution(794505036848824269)
XLA Ops:
  19.0 11.5 %all-to-all-start = ((f32[32,1,1]{2,1,0:T(1,128)}), f32[32,1,1]{2,1,0:T(1,128)}, u32[]{:S(2)}, u32[]{:S(2)}) async-start(f32[32,1,1]{2,1,0:T(1,128)} %copy.715), calls=%async_computation | async-start | bytes 32768 | tf_op jit(solution)/shard_map/all_to_all | solution.py:152
  35.8 3.9 slice.193
  43.6 3.7 reshape.1148
  47.3 3.8 bitcast_reduce_fusion
  56.5 4.7 copy.728
  61.2 4.6 reshape.1155
  79.7 2.8 slice.202
  82.5 2.8 slice.198
  140.6 2.8 gather_fusion.23
  179.1 67.7 %all-gather.11.cloned.1.call-done = bf16[4096,1,384]{2,0,1:T(8,128)(2,1)} async-done(((bf16[128,1,384]{2,0,1:T(8,128)(2,1)}), bf16[4096,1,384]{2,0,1:T(8,128)(2,1)}) %all-gather.11.cloned.1.call-update) | async-done | bytes 3145744 | tf_op jit(solution)/shard_map/all_gather | solution.py:135
  254.5 3.3 fusion.162
  259.4 3.4 fusion.164
  270.3 3.3 convolution_bitcast_fusion.2
  277.1 46.8 %all-gather.5.cloned.1.call-done = bf16[4096,1,384]{2,0,1:T(8,128)(2,1)} async-done(((bf16[128,1,384]{2,0,1:T(8,128)(2,1)}), bf16[4096,1,384]{2,0,1:T(8,128)(2,1)}) %all-gather.5.cloned.1.call-update) | async-done | bytes 3145744 | tf_op jit(solution)/shard_map/all_gather | solution.py:135
  372.1 5.6 all-to-all-start.1
  377.7 3.2 convolution_bitcast_fusion.4
  400.3 9.2 %all-to-all-start.4 = ((f32[32,1,8,1,6]{2,3,4,1,0:T(1,128)}), f32[32,1,8,1,6]{2,3,4,1,0:T(1,128)S(1)}, u32[]{:S(2)}, u32[]{:S(2)}) async-start(f32[32,1,8,1,6]{2,3,4,1,0:T(1,128)} %copy.745), calls=%async_computation.4 | async-start | bytes 196608 | tf_op jit(solution)/shard_map/all_to_all | solution.py:163
  409.5 2.7 fusion.69
  418.4 8.4 all-to-all-start.7
  426.9 8.7 %all-to-all-done.7 = f32[32,1,8,1,6]{2,3,4,1,0:T(1,128)S(1)} async-done(((f32[32,1,8,1,6]{2,3,4,1,0:T(1,128)}), f32[32,1,8,1,6]{2,3,4,1,0:T(1,128)S(1)}, u32[]{:S(2)}, u32[]{:S(2)}) %all-to-all-start.7) | async-done | bytes 6176 | tf_op jit(solution)/shard_map/all_to_all | solution.py:163
  435.6 4.3 all-to-all-start.10
  441.5 6.9 all-to-all-done.10
  448.4 3.8 all-to-all-start.3
  453.8 7.3 all-to-all-done.3
  461.1 3.8 all-to-all-start.12
  465.9 8.0 all-to-all-done.12
  473.9 4.5 all-to-all-start.6
  481.4 5.9 all-to-all-done.6
  487.3 4.5 all-to-all-start.9
  503.8 9.2 %all-to-all-start.2 = ((f32[32,1,8,1,384]{4,2,3,1,0:T(8,128)}), f32[32,1,8,1,384]{4,2,3,1,0:T(8,128)S(1)}, u32[]{:S(2)}, u32[]{:S(2)}) async-start(f32[32,1,8,1,384]{4,2,3,1,0:T(8,128)} %get-tuple-element.103), calls=%async_computation.2 | async-start | bytes 786432 | tf_op jit(solution)/shard_map/all_to_all | solution.py:189
  530.5 7.8 exponential_select_fusion.1
  539.5 9.3 %all-to-all-start.5 = ((f32[32,1,8,1,384]{4,2,3,1,0:T(8,128)}), f32[32,1,8,1,384]{4,2,3,1,0:T(8,128)}, u32[]{:S(2)}, u32[]{:S(2)}) async-start(f32[32,1,8,1,384]{4,2,3,1,0:T(8,128)} %get-tuple-element.101), calls=%async_computation.5 | async-start | bytes 786432 | tf_op jit(solution)/shard_map/all_to_all | solution.py:189
  552.9 7.7 multiply_reduce_fusion.3
  561.9 9.2 %all-to-all-start.11 = ((f32[32,1,8,1,384]{4,2,3,1,0:T(8,128)}), f32[32,1,8,1,384]{4,2,3,1,0:T(8,128)S(1)}, u32[]{:S(2)}, u32[]{:S(2)}) async-start(f32[32,1,8,1,384]{4,2,3,1,0:T(8,128)} %get-tuple-element.102), calls=%async_computation.11 | async-start | bytes 786432 | tf_op jit(solution)/shard_map/all_to_all | solution.py:189
  577.7 7.7 multiply_reduce_fusion.2
  590.9 9.3 %all-to-all-start.8 = ((f32[32,1,8,1,384]{4,2,3,1,0:T(8,128)}), f32[32,1,8,1,384]{4,2,3,1,0:T(8,128)}, u32[]{:S(2)}, u32[]{:S(2)}) async-start(f32[32,1,8,1,384]{4,2,3,1,0:T(8,128)} %get-tuple-element.100), calls=%async_computation.8 | async-start | bytes 786432 | tf_op jit(solution)/shard_map/all_to_all | solution.py:189
  604.5 7.7 multiply_reduce_fusion
  620.3 7.7 multiply_reduce_fusion.1
  631.2 88.7 %all-reduce.7.cloned.1.call-done = (f32[128,1536]{1,0:T(8,128)}, f32[128,1536]{1,0:T(8,128)}, f32[128,1536]{1,0:T(8,128)}, f32[128,1536]{1,0:T(8,128)}) async-done(((f32[128,1536]{1,0:T(8,128)}, f32[128,1536]{1,0:T(8,128)}, f32[128,1536]{1,0:T(8,128)}, f32[128,1536]{1,0:T(8,128)}), (f32[128,1536]{1,0:T(8,128)}, f32[128,1536]{1,0:T(8,128)}, f32[128,1536]{1,0:T(8,128)}, ...) | async-done | bytes 3145744 | tf_op jit(solution)/shard_map/psum | solution.py:238
  719.9 3.0 multiply_reduce_fusion.10
  728.4 4.1 fusion.33
  732.5 4.1 fusion.34
  736.5 3.4 fusion.169
  739.9 4.1 fusion.35
  744.1 3.3 fusion.167
  747.3 4.0 fusion.36
  751.3 76.1 %all-reduce.5.cloned.1.call-done = (f32[128,1536]{1,0:T(8,128)}, f32[128,1536]{1,0:T(8,128)}, f32[128,1536]{1,0:T(8,128)}, f32[128,1536]{1,0:T(8,128)}) async-done(((f32[128,1536]{1,0:T(8,128)}, f32[128,1536]{1,0:T(8,128)}, f32[128,1536]{1,0:T(8,128)}, f32[128,1536]{1,0:T(8,128)}), (f32[128,1536]{1,0:T(8,128)}, f32[128,1536]{1,0:T(8,128)}, f32[128,1536]{1,0:T(8,128)}, ...) | async-done | bytes 3145744 | tf_op jit(solution)/shard_map/psum | solution.py:244
  827.4 4.1 fusion.58
  (463 shorter events, 302.6 us)
Async XLA Ops:
  6.5 721.9 %copy-start = (bf16[1024,1536]{1,0:T(8,128)(2,1)S(1)}, bf16[1024,1536]{1,0:T(8,128)(2,1)}, u32[]{:S(2)}) copy-start(bf16[1024,1536]{1,0:T(8,128)(2,1)} %param.35) | copy-start | bytes 9437188
  6.5 165.9 %all-gather.9.cloned.1.call-start = ((), (), s32[]{:S(2)}) async-start(), calls=%async_computation.15 | async-start | bytes 3244032 | tf_op jit(solution)/shard_map/all_gather | solution.py:135
  15.1 160.7 %all-gather.7.cloned.1.call-start = ((), (), s32[]{:S(2)}) async-start(), calls=%async_computation.14 | async-start | bytes 3244032 | tf_op jit(solution)/shard_map/all_gather | solution.py:135
  15.8 231.1 %all-gather.11.cloned.1.call-start = ((), (), s32[]{:S(2)}) async-start(), calls=%async_computation.16 | async-start | bytes 3244032 | tf_op jit(solution)/shard_map/all_gather | solution.py:135
  17.6 17.3 %copy-start.87 = (pred[16]{0:T(512)(128)(4,1)}, pred[16]{0:T(512)(128)(4,1)S(1)}, u32[]{:S(2)}) copy-start(pred[16]{0:T(512)(128)(4,1)S(1)} %broadcast_compare_fusion) | copy-start | bytes 52
  19.0 150.7 %all-to-all-start = ((f32[32,1,1]{2,1,0:T(1,128)}), f32[32,1,1]{2,1,0:T(1,128)}, u32[]{:S(2)}, u32[]{:S(2)}) async-start(f32[32,1,1]{2,1,0:T(1,128)} %copy.715), calls=%async_computation | async-start | bytes 32768 | tf_op jit(solution)/shard_map/all_to_all | solution.py:152
  30.4 293.4 %all-gather.5.cloned.1.call-start = ((), (), s32[]{:S(2)}) async-start(), calls=%async_computation.13 | async-start | bytes 3244032 | tf_op jit(solution)/shard_map/all_gather | solution.py:135
  87.7 21.9 %copy-start.39 = (f32[32,8,1,6]{1,2,3,0:T(1,128)S(1)}, f32[32,8,1,6]{1,2,3,0:T(1,128)}, u32[]{:S(2)}) copy-start(f32[32,8,1,6]{1,2,3,0:T(1,128)} %get-tuple-element.76) | copy-start | bytes 18436
  105.5 19.6 %copy-start.69 = (f32[128,6]{0,1:T(8,128)S(1)}, f32[128,6]{0,1:T(8,128)}, u32[]{:S(2)}) copy-start(f32[128,6]{0,1:T(8,128)} %copy.815) | copy-start | bytes 9220
  106.5 20.0 %copy-start.53 = (f32[128,6]{0,1:T(8,128)S(1)}, f32[128,6]{0,1:T(8,128)}, u32[]{:S(2)}) copy-start(f32[128,6]{0,1:T(8,128)} %slice_add_fusion.1) | copy-start | bytes 9220
  140.6 14.2 %copy-start.33 = (bf16[2,128,384]{1,2,0:T(8,128)(2,1)S(1)}, bf16[2,128,384]{1,2,0:T(8,128)(2,1)}, u32[]{:S(2)}) copy-start(bf16[2,128,384]{1,2,0:T(8,128)(2,1)} %copy.782) | copy-start | bytes 589828
  148.1 18.0 %copy-start.79 = (s32[16]{0:T(128)S(1)}, s32[16]{0:T(128)}, u32[]{:S(2)}) copy-start(s32[16]{0:T(128)} %copy-done.78) | copy-start | bytes 196
  166.1 226.7 %copy-start.56 = (s32[1024]{0:T(1024)}, s32[1024]{0:T(1024)S(1)}, u32[]{:S(2)}) copy-start(s32[1024]{0:T(1024)S(1)} %pad_clamp_fusion.3) | copy-start | bytes 12292
  264.4 10.9 %copy-start.30 = (f32[16,8,6]{1,2,0:T(8,128)S(1)}, f32[16,8,6]{1,2,0:T(8,128)}, u32[]{:S(2)}) copy-start(f32[16,8,6]{1,2,0:T(8,128)} %get-tuple-element.119) | copy-start | bytes 9220
  327.2 41.9 %copy-start.81 = (pred[32]{0:T(512)(128)(4,1)S(1)}, pred[32]{0:T(512)(128)(4,1)}, u32[]{:S(2)}) copy-start(pred[32]{0:T(512)(128)(4,1)} %fusion.115) | copy-start | bytes 100
  372.1 28.2 %all-to-all-start.1 = ((f32[32,1,8,1,6]{2,3,4,1,0:T(1,128)}), f32[32,1,8,1,6]{2,3,4,1,0:T(1,128)}, u32[]{:S(2)}, u32[]{:S(2)}) async-start(f32[32,1,8,1,6]{2,3,4,1,0:T(1,128)} %copy.724), calls=%async_computation.1 | async-start | bytes 196608 | tf_op jit(solution)/shard_map/all_to_all | solution.py:163
  388.3 21.1 %copy-start.82 = (pred[32]{0:T(512)(128)(4,1)S(1)}, pred[32]{0:T(512)(128)(4,1)}, u32[]{:S(2)}) copy-start(pred[32]{0:T(512)(128)(4,1)} %fusion.115) | copy-start | bytes 100
  394.1 19.5 %copy-start.49 = (f32[32,1,8,1,6]{0,2,4,3,1:T(8,128)S(1)}, f32[32,1,8,1,6]{0,2,4,3,1:T(8,128)}, u32[]{:S(2)}) copy-start(f32[32,1,8,1,6]{0,2,4,3,1:T(8,128)} %get-tuple-element.110) | copy-start | bytes 18436
  394.1 20.3 %copy-start.48 = (f32[32,1,8,1,6]{0,2,4,3,1:T(8,128)S(1)}, f32[32,1,8,1,6]{0,2,4,3,1:T(8,128)}, u32[]{:S(2)}) copy-start(f32[32,1,8,1,6]{0,2,4,3,1:T(8,128)} %get-tuple-element.107) | copy-start | bytes 18436
  394.1 21.0 %copy-start.47 = (f32[32,1,8,1,6]{0,2,4,3,1:T(8,128)S(1)}, f32[32,1,8,1,6]{0,2,4,3,1:T(8,128)}, u32[]{:S(2)}) copy-start(f32[32,1,8,1,6]{0,2,4,3,1:T(8,128)} %get-tuple-element.109) | copy-start | bytes 18436
  394.1 21.7 %copy-start.46 = (f32[32,1,8,1,6]{0,2,4,3,1:T(8,128)S(1)}, f32[32,1,8,1,6]{0,2,4,3,1:T(8,128)}, u32[]{:S(2)}) copy-start(f32[32,1,8,1,6]{0,2,4,3,1:T(8,128)} %get-tuple-element.104) | copy-start | bytes 18436
  396.0 30.8 %copy-start.44 = (f32[32,8,1,6]{0,1,3,2:T(8,128)S(1)}, f32[32,8,1,6]{0,1,3,2:T(8,128)}, u32[]{:S(2)}) copy-start(f32[32,8,1,6]{0,1,3,2:T(8,128)} %copy.726) | copy-start | bytes 18436
  396.0 30.8 %copy-start.45 = (f32[32,8,1,6]{0,1,3,2:T(8,128)S(1)}, f32[32,8,1,6]{0,1,3,2:T(8,128)}, u32[]{:S(2)}) copy-start(f32[32,8,1,6]{0,1,3,2:T(8,128)} %copy.747) | copy-start | bytes 18436
  397.2 55.7 %copy-start.42 = (f32[32,8,1,6]{0,1,3,2:T(8,128)S(1)}, f32[32,8,1,6]{0,1,3,2:T(8,128)}, u32[]{:S(2)}) copy-start(f32[32,8,1,6]{0,1,3,2:T(8,128)} %copy.773) | copy-start | bytes 18436
  397.2 55.7 %copy-start.43 = (f32[32,8,1,6]{0,1,3,2:T(8,128)S(1)}, f32[32,8,1,6]{0,1,3,2:T(8,128)}, u32[]{:S(2)}) copy-start(f32[32,8,1,6]{0,1,3,2:T(8,128)} %copy.805) | copy-start | bytes 18436
  398.8 13.4 %copy-start.51 = (f32[32,1,8,1,6]{0,2,4,3,1:T(8,128)S(1)}, f32[32,1,8,1,6]{0,2,4,3,1:T(8,128)}, u32[]{:S(2)}) copy-start(f32[32,1,8,1,6]{0,2,4,3,1:T(8,128)} %get-tuple-element.105) | copy-start | bytes 18436
  398.8 14.1 %copy-start.50 = (f32[32,1,8,1,6]{0,2,4,3,1:T(8,128)S(1)}, f32[32,1,8,1,6]{0,2,4,3,1:T(8,128)}, u32[]{:S(2)}) copy-start(f32[32,1,8,1,6]{0,2,4,3,1:T(8,128)} %get-tuple-element.108) | copy-start | bytes 18436
  400.3 18.1 %all-to-all-start.4 = ((f32[32,1,8,1,6]{2,3,4,1,0:T(1,128)}), f32[32,1,8,1,6]{2,3,4,1,0:T(1,128)S(1)}, u32[]{:S(2)}, u32[]{:S(2)}) async-start(f32[32,1,8,1,6]{2,3,4,1,0:T(1,128)} %copy.745), calls=%async_computation.4 | async-start | bytes 196608 | tf_op jit(solution)/shard_map/all_to_all | solution.py:163
  418.4 17.3 %all-to-all-start.7 = ((f32[32,1,8,1,6]{2,3,4,1,0:T(1,128)}), f32[32,1,8,1,6]{2,3,4,1,0:T(1,128)S(1)}, u32[]{:S(2)}, u32[]{:S(2)}) async-start(f32[32,1,8,1,6]{2,3,4,1,0:T(1,128)} %copy.771), calls=%async_computation.7 | async-start | bytes 196608 | tf_op jit(solution)/shard_map/all_to_all | solution.py:163
  426.9 76.8 %copy-start.34 = (f32[64,8,6]{0,1,2:T(8,128)}, f32[64,8,6]{0,1,2:T(8,128)S(1)}, u32[]{:S(2)}) copy-start(f32[64,8,6]{0,1,2:T(8,128)S(1)} %get-tuple-element.124) | copy-start | bytes 36868
  435.6 12.7 %all-to-all-start.10 = ((f32[32,1,8,1,6]{2,3,4,1,0:T(1,128)}), f32[32,1,8,1,6]{2,3,4,1,0:T(1,128)S(1)}, u32[]{:S(2)}, u32[]{:S(2)}) async-start(f32[32,1,8,1,6]{2,3,4,1,0:T(1,128)} %copy.803), calls=%async_computation.10 | async-start | bytes 196608 | tf_op jit(solution)/shard_map/all_to_all | solution.py:163
  440.8 62.9 %copy-start.27 = (f32[16,8,6]{1,2,0:T(8,128)}, f32[16,8,6]{1,2,0:T(8,128)S(1)}, u32[]{:S(2)}) copy-start(f32[16,8,6]{1,2,0:T(8,128)S(1)} %select_reduce_fusion.3) | copy-start | bytes 9220
  448.4 12.7 %all-to-all-start.3 = ((f32[32,1,8,1,6]{2,3,4,1,0:T(1,128)}), f32[32,1,8,1,6]{2,3,4,1,0:T(1,128)S(1)}, u32[]{:S(2)}, u32[]{:S(2)}) async-start(f32[32,1,8,1,6]{2,3,4,1,0:T(1,128)} %copy.737), calls=%async_computation.3 | async-start | bytes 196608 | tf_op jit(solution)/shard_map/all_to_all | solution.py:176
  453.7 50.0 %copy-start.35 = (f32[64,8,6]{0,1,2:T(8,128)}, f32[64,8,6]{0,1,2:T(8,128)S(1)}, u32[]{:S(2)}) copy-start(f32[64,8,6]{0,1,2:T(8,128)S(1)} %get-tuple-element.125) | copy-start | bytes 36868
  453.8 50.0 %copy-start.36 = (f32[64,8,6]{0,1,2:T(8,128)}, f32[64,8,6]{0,1,2:T(8,128)S(1)}, u32[]{:S(2)}) copy-start(f32[64,8,6]{0,1,2:T(8,128)S(1)} %get-tuple-element.126) | copy-start | bytes 36868
  461.1 12.8 %all-to-all-start.12 = ((f32[32,1,8,1,6]{2,3,4,1,0:T(1,128)}), f32[32,1,8,1,6]{2,3,4,1,0:T(1,128)S(1)}, u32[]{:S(2)}, u32[]{:S(2)}) async-start(f32[32,1,8,1,6]{2,3,4,1,0:T(1,128)} %copy.826), calls=%async_computation.12 | async-start | bytes 196608 | tf_op jit(solution)/shard_map/all_to_all | solution.py:176
  473.9 13.4 %all-to-all-start.6 = ((f32[32,1,8,1,6]{2,3,4,1,0:T(1,128)}), f32[32,1,8,1,6]{2,3,4,1,0:T(1,128)}, u32[]{:S(2)}, u32[]{:S(2)}) async-start(f32[32,1,8,1,6]{2,3,4,1,0:T(1,128)} %copy.763), calls=%async_computation.6 | async-start | bytes 196608 | tf_op jit(solution)/shard_map/all_to_all | solution.py:176
  480.4 23.4 %copy-start.24 = (f32[16,8,6]{1,2,0:T(8,128)}, f32[16,8,6]{1,2,0:T(8,128)S(1)}, u32[]{:S(2)}) copy-start(f32[16,8,6]{1,2,0:T(8,128)S(1)} %get-tuple-element.10) | copy-start | bytes 9220
  480.4 23.4 %copy-start.25 = (f32[16,8,6]{1,2,0:T(8,128)}, f32[16,8,6]{1,2,0:T(8,128)S(1)}, u32[]{:S(2)}) copy-start(f32[16,8,6]{1,2,0:T(8,128)S(1)} %get-tuple-element.11) | copy-start | bytes 9220
  480.4 23.4 %copy-start.26 = (f32[16,8,6]{1,2,0:T(8,128)}, f32[16,8,6]{1,2,0:T(8,128)S(1)}, u32[]{:S(2)}) copy-start(f32[16,8,6]{1,2,0:T(8,128)S(1)} %get-tuple-element.12) | copy-start | bytes 9220
  487.3 16.4 %all-to-all-start.9 = ((f32[32,1,8,1,6]{2,3,4,1,0:T(1,128)}), f32[32,1,8,1,6]{2,3,4,1,0:T(1,128)}, u32[]{:S(2)}, u32[]{:S(2)}) async-start(f32[32,1,8,1,6]{2,3,4,1,0:T(1,128)} %copy.794), calls=%async_computation.9 | async-start | bytes 196608 | tf_op jit(solution)/shard_map/all_to_all | solution.py:176
  503.8 35.7 %all-to-all-start.2 = ((f32[32,1,8,1,384]{4,2,3,1,0:T(8,128)}), f32[32,1,8,1,384]{4,2,3,1,0:T(8,128)S(1)}, u32[]{:S(2)}, u32[]{:S(2)}) async-start(f32[32,1,8,1,384]{4,2,3,1,0:T(8,128)} %get-tuple-element.103), calls=%async_computation.2 | async-start | bytes 786432 | tf_op jit(solution)/shard_map/all_to_all | solution.py:189
  539.5 22.4 %all-to-all-start.5 = ((f32[32,1,8,1,384]{4,2,3,1,0:T(8,128)}), f32[32,1,8,1,384]{4,2,3,1,0:T(8,128)}, u32[]{:S(2)}, u32[]{:S(2)}) async-start(f32[32,1,8,1,384]{4,2,3,1,0:T(8,128)} %get-tuple-element.101), calls=%async_computation.5 | async-start | bytes 786432 | tf_op jit(solution)/shard_map/all_to_all | solution.py:189
  561.9 28.9 %all-to-all-start.11 = ((f32[32,1,8,1,384]{4,2,3,1,0:T(8,128)}), f32[32,1,8,1,384]{4,2,3,1,0:T(8,128)S(1)}, u32[]{:S(2)}, u32[]{:S(2)}) async-start(f32[32,1,8,1,384]{4,2,3,1,0:T(8,128)} %get-tuple-element.102), calls=%async_computation.11 | async-start | bytes 786432 | tf_op jit(solution)/shard_map/all_to_all | solution.py:189
  590.9 24.4 %all-to-all-start.8 = ((f32[32,1,8,1,384]{4,2,3,1,0:T(8,128)}), f32[32,1,8,1,384]{4,2,3,1,0:T(8,128)}, u32[]{:S(2)}, u32[]{:S(2)}) async-start(f32[32,1,8,1,384]{4,2,3,1,0:T(8,128)} %get-tuple-element.100), calls=%async_computation.8 | async-start | bytes 786432 | tf_op jit(solution)/shard_map/all_to_all | solution.py:189
  600.2 119.6 %all-reduce.7.cloned.1.call-start = ((), (), s32[]{:S(2)}) async-start(), calls=%async_computation.18 | async-start | bytes 6291456 | tf_op jit(solution)/shard_map/psum | solution.py:238
  631.1 91.7 %copy-start.76 = (f32[1536]{0:T(1024)S(1)}, f32[1536]{0:T(1024)}, u32[]{:S(2)}) copy-start(f32[1536]{0:T(1024)} %param.32) | copy-start | bytes 18436
  631.1 196.3 %all-reduce.5.cloned.1.call-start = ((), (), s32[]{:S(2)}) async-start(), calls=%async_computation.17 | async-start | bytes 6291456 | tf_op jit(solution)/shard_map/psum | solution.py:244
  (63 other events, 326.7 us)
Sparse Core Ops, SparseCore 0:
  15.2 77.4 all-gather.8
  95.7 74.0 all-gather.6
  172.8 74.0 all-gather.10
  249.7 74.0 all-gather.4
  631.3 88.5 all-reduce.6
  751.5 75.9 all-reduce.4
where the time goes:
time: 854 us; the launch traced here: 840 us
  waiting for transfers between devices  319 us (37%)
  local copies, waits for them, and re-layouts  223 us (26%)
  other arithmetic  123 us (14%)
  starting transfers between devices  93.1 us (11%)
  matrix products  66.5 us (8%)
  between operations  14.9 us (2%)
    all_gather x4, waiting for transfers between devices, shards(): gathered = lax.all_gather(query_block, 'group', axis=0, tiled=True)  115 us
    psum x1, waiting for transfers between devices, shards(): lax.psum(jnp.dot(attended, w_out, preferred_element_type=jnp.float32), 'h...  88.7 us
    psum x1, waiting for transfers between devices, shards(): lax.psum(jnp.dot(hidden, w_down, preferred_element_type=jnp.float32), 'he...  76.1 us
    all_to_all x4, starting transfers between devices, shards(): lax.all_to_all(jnp.where(full_slot, numerator[slot_source], 0.0), 'group'...  37 us
    reduce_sum x4, other arithmetic, by_request(): combined = jnp.sum(factor[..., None] * numer_split[None], axis=1)  30.9 us
    all_to_all x4, starting transfers between devices, shards(): lax.all_to_all(jnp.where(full_slot, page_top[slot_source], masked_score),...  27.4 us
    all_to_all x4, waiting for transfers between devices, shards(): lax.all_to_all(jnp.where(full_slot, page_total[slot_source], 0.0), 'group...  21.2 us
  transfers between devices with their start and end apart: 19, of which 11 were waited for; matrix products, arithmetic and copies ran while one was open for 36% of the time, Pallas kernels for 0%

commit v1 on v0

--- a/solution.py
+++ b/solution.py
@@ -132,7 +132,9 @@
     for step_index in range(step_count):
         query_block = by_row[:, step_index : step_index + 1]
         step_span = query_block.shape[1]
-        gathered = lax.all_gather(query_block, "group", axis=0, tiled=True)
+        gathered = jnp.concatenate(
+            lax.all_to_all(jnp.stack([query_block] * lax.axis_size("group")), "group", 0, 0), axis=0
+        )
         asked_rows = gathered.reshape(groups * local_count, BEAMS, step_span, inner_width)[
             hosted_request
         ]

time: 854 us -> 813 us (0.952)
  waiting for transfers between devices: 319 us -> 225 us
  starting transfers between devices: 93.1 us -> 129 us
  local copies, waits for them, and re-layouts: 223 us -> 239 us
    all_gather x4 -> x0, waiting for transfers between devices: 115 us -> none  [shards(): gathered = lax.all_gather(query_block, 'group', axis=0, tiled=True)]
    all_to_all x0 -> x4, starting transfers between devices: none -> 33.7 us  [shards(): lax.all_to_all(jnp.stack([query_block] * lax.axis_size('group')), 'group'...]
    all_to_all x0 -> x4, waiting for transfers between devices: none -> 23.5 us  [shards(): lax.all_to_all(jnp.stack([query_block] * lax.axis_size('group')), 'group'...]
    another operation x4 -> x8, local copies, waits for them, and re-layouts: 3.51 us -> 14.9 us  [the longest x4 11.4 us: shards(): jnp.stack([query_block] * lax.axis_size('group'))]
  transfers between devices with their start and end apart: 19 -> 19, of which waited for: 11 -> 11; matrix products, arithmetic and copies ran while one was open for 36% -> 39% of each run, Pallas kernels for 0% -> 0%
where the time goes in v1:
time: 813 us; the launch traced here: 801 us
  local copies, waits for them, and re-layouts  239 us (29%)
  waiting for transfers between devices  225 us (28%)
  starting transfers between devices  129 us (16%)
  other arithmetic  119 us (15%)
  matrix products  72.7 us (9%)
  between operations  14.9 us (2%)
    psum x1, waiting for transfers between devices, shards(): lax.psum(jnp.dot(attended, w_out, preferred_element_type=jnp.float32), 'h...  87.6 us
    psum x1, waiting for transfers between devices, shards(): lax.psum(jnp.dot(hidden, w_down, preferred_element_type=jnp.float32), 'he...  76.1 us
    all_to_all x4, starting transfers between devices, shards(): lax.all_to_all(jnp.where(full_slot, numerator[slot_source], 0.0), 'group'...  37 us
    all_to_all x4, starting transfers between devices, shards(): lax.all_to_all(jnp.stack([query_block] * lax.axis_size('group')), 'group'...  33.7 us
    reduce_sum x4, other arithmetic, by_request(): combined = jnp.sum(factor[..., None] * numer_split[None], axis=1)  30.9 us
    all_to_all x4, starting transfers between devices, shards(): lax.all_to_all(jnp.where(full_slot, page_top[slot_source], masked_score),...  30.1 us
    all_to_all x4, waiting for transfers between devices, shards(): lax.all_to_all(jnp.stack([query_block] * lax.axis_size('group')), 'group'...  23.5 us
    all_to_all x4, waiting for transfers between devices, shards(): lax.all_to_all(jnp.where(full_slot, page_total[slot_source], 0.0), 'group...  21.3 us
  transfers between devices with their start and end apart: 19, of which 11 were waited for; matrix products, arithmetic and copies ran while one was open for 39% of the time, Pallas kernels for 0%

profile of v1, /device:TPU:1, one launch (start us, length us, event | category | flops | bytes accessed | tf_op | source)
XLA Modules:
  0.0 800.7 jit_solution(6131655672038056932)
XLA Ops:
  9.8 11.3 %all-to-all-start = ((f32[32,1,1]{2,1,0:T(1,128)}), f32[32,1,1]{2,1,0:T(1,128)S(1)}, u32[]{:S(2)}, u32[]{:S(2)}) async-start(f32[32,1,1]{2,1,0:T(1,128)} %copy.719), calls=%async_computation | async-start | bytes 32768 | tf_op jit(solution)/shard_map/all_to_all | solution.py:154
  32.6 9.3 %all-to-all-start.9 = ((bf16[32,128,1,384]{3,1,2,0:T(8,128)(2,1)}), bf16[32,128,1,384]{3,1,2,0:T(8,128)(2,1)}, u32[]{:S(2)}, u32[]{:S(2)}) async-start(bf16[32,128,1,384]{3,1,2,0:T(8,128)(2,1)} %stack.22), calls=%async_computation.9 | async-start | bytes 6291456 | tf_op jit(solution)/shard_map/all_to_all | solution.py:136
  43.6 4.0 slice.201
  51.5 3.8 reshape.1148
  58.2 3.8 bitcast_reduce_fusion
  63.8 3.5 convolution_bitcast_fusion
  67.2 14.7 %all-to-all-done.9 = bf16[32,128,1,384]{3,1,2,0:T(8,128)(2,1)} async-done(((bf16[32,128,1,384]{3,1,2,0:T(8,128)(2,1)}), bf16[32,128,1,384]{3,1,2,0:T(8,128)(2,1)}, u32[]{:S(2)}, u32[]{:S(2)}) %all-to-all-start.9) | async-done | bytes 3145760 | tf_op jit(solution)/shard_map/all_to_all | solution.py:136
  84.2 7.4 all-to-all-start.5
  92.2 6.6 copy.732
  98.8 4.5 reshape.1154
  123.9 7.5 all-to-all-done.5
  134.6 7.3 all-to-all-start.13
  232.9 9.7 %all-to-all-start.1 = ((bf16[32,128,1,384]{3,1,2,0:T(8,128)(2,1)}), bf16[32,128,1,384]{3,1,2,0:T(8,128)(2,1)}, u32[]{:S(2)}, u32[]{:S(2)}) async-start(bf16[32,128,1,384]{3,1,2,0:T(8,128)(2,1)} %stack.18), calls=%async_computation.1 | async-start | bytes 6291456 | tf_op jit(solution)/shard_map/all_to_all | solution.py:136
  258.4 3.3 fusion.161
  263.3 3.3 fusion.163
  274.2 3.3 convolution_bitcast_fusion.2
  330.6 8.2 %all-to-all-start.2 = ((f32[32,1,8,1,6]{2,3,4,1,0:T(1,128)}), f32[32,1,8,1,6]{2,3,4,1,0:T(1,128)}, u32[]{:S(2)}, u32[]{:S(2)}) async-start(f32[32,1,8,1,6]{2,3,4,1,0:T(1,128)} %copy.728), calls=%async_computation.2 | async-start | bytes 196608 | tf_op jit(solution)/shard_map/all_to_all | solution.py:165
  338.9 3.2 convolution_bitcast_fusion.4
  361.5 9.2 %all-to-all-start.6 = ((f32[32,1,8,1,6]{2,3,4,1,0:T(1,128)}), f32[32,1,8,1,6]{2,3,4,1,0:T(1,128)S(1)}, u32[]{:S(2)}, u32[]{:S(2)}) async-start(f32[32,1,8,1,6]{2,3,4,1,0:T(1,128)} %copy.749), calls=%async_computation.6 | async-start | bytes 196608 | tf_op jit(solution)/shard_map/all_to_all | solution.py:165
  379.6 8.4 %all-to-all-start.10 = ((f32[32,1,8,1,6]{2,3,4,1,0:T(1,128)}), f32[32,1,8,1,6]{2,3,4,1,0:T(1,128)S(1)}, u32[]{:S(2)}, u32[]{:S(2)}) async-start(f32[32,1,8,1,6]{2,3,4,1,0:T(1,128)} %copy.775), calls=%async_computation.10 | async-start | bytes 196608 | tf_op jit(solution)/shard_map/all_to_all | solution.py:165
  388.2 8.7 %all-to-all-done.10 = f32[32,1,8,1,6]{2,3,4,1,0:T(1,128)S(1)} async-done(((f32[32,1,8,1,6]{2,3,4,1,0:T(1,128)}), f32[32,1,8,1,6]{2,3,4,1,0:T(1,128)S(1)}, u32[]{:S(2)}, u32[]{:S(2)}) %all-to-all-start.10) | async-done | bytes 6176 | tf_op jit(solution)/shard_map/all_to_all | solution.py:165
  396.9 4.3 all-to-all-start.14
  402.7 7.4 all-to-all-done.14
  410.1 3.8 all-to-all-start.4
  415.5 7.3 all-to-all-done.4
  422.9 3.8 all-to-all-start.16
  427.6 8.0 all-to-all-done.16
  435.6 4.6 all-to-all-start.8
  443.1 5.9 all-to-all-done.8
  449.1 4.6 all-to-all-start.12
  465.6 9.2 %all-to-all-start.3 = ((f32[32,1,8,1,384]{4,2,3,1,0:T(8,128)}), f32[32,1,8,1,384]{4,2,3,1,0:T(8,128)S(1)}, u32[]{:S(2)}, u32[]{:S(2)}) async-start(f32[32,1,8,1,384]{4,2,3,1,0:T(8,128)} %get-tuple-element.103), calls=%async_computation.3 | async-start | bytes 786432 | tf_op jit(solution)/shard_map/all_to_all | solution.py:191
  492.3 7.8 exponential_select_fusion.1
  501.4 9.3 %all-to-all-start.7 = ((f32[32,1,8,1,384]{4,2,3,1,0:T(8,128)}), f32[32,1,8,1,384]{4,2,3,1,0:T(8,128)}, u32[]{:S(2)}, u32[]{:S(2)}) async-start(f32[32,1,8,1,384]{4,2,3,1,0:T(8,128)} %get-tuple-element.101), calls=%async_computation.7 | async-start | bytes 786432 | tf_op jit(solution)/shard_map/all_to_all | solution.py:191
  514.7 7.7 multiply_reduce_fusion.3
  523.8 9.2 %all-to-all-start.15 = ((f32[32,1,8,1,384]{4,2,3,1,0:T(8,128)}), f32[32,1,8,1,384]{4,2,3,1,0:T(8,128)S(1)}, u32[]{:S(2)}, u32[]{:S(2)}) async-start(f32[32,1,8,1,384]{4,2,3,1,0:T(8,128)} %get-tuple-element.102), calls=%async_computation.15 | async-start | bytes 786432 | tf_op jit(solution)/shard_map/all_to_all | solution.py:191
  539.6 7.7 multiply_reduce_fusion.2
  552.7 9.3 %all-to-all-start.11 = ((f32[32,1,8,1,384]{4,2,3,1,0:T(8,128)}), f32[32,1,8,1,384]{4,2,3,1,0:T(8,128)}, u32[]{:S(2)}, u32[]{:S(2)}) async-start(f32[32,1,8,1,384]{4,2,3,1,0:T(8,128)} %get-tuple-element.100), calls=%async_computation.11 | async-start | bytes 786432 | tf_op jit(solution)/shard_map/all_to_all | solution.py:191
  566.3 7.7 multiply_reduce_fusion
  582.1 7.7 multiply_reduce_fusion.1
  593.1 87.6 %all-reduce.7.cloned.1.call-done = (f32[128,1536]{1,0:T(8,128)}, f32[128,1536]{1,0:T(8,128)}, f32[128,1536]{1,0:T(8,128)}, f32[128,1536]{1,0:T(8,128)}) async-done(((f32[128,1536]{1,0:T(8,128)}, f32[128,1536]{1,0:T(8,128)}, f32[128,1536]{1,0:T(8,128)}, f32[128,1536]{1,0:T(8,128)}), (f32[128,1536]{1,0:T(8,128)}, f32[128,1536]{1,0:T(8,128)}, f32[128,1536]{1,0:T(8,128)}, ...) | async-done | bytes 3145744 | tf_op jit(solution)/shard_map/psum | solution.py:240
  689.2 4.1 fusion.33
  693.2 4.1 fusion.34
  697.3 3.4 fusion.168
  700.7 4.1 fusion.35
  704.8 3.3 fusion.166
  708.1 4.0 fusion.36
  712.1 76.1 %all-reduce.5.cloned.1.call-done = (f32[128,1536]{1,0:T(8,128)}, f32[128,1536]{1,0:T(8,128)}, f32[128,1536]{1,0:T(8,128)}, f32[128,1536]{1,0:T(8,128)}) async-done(((f32[128,1536]{1,0:T(8,128)}, f32[128,1536]{1,0:T(8,128)}, f32[128,1536]{1,0:T(8,128)}, f32[128,1536]{1,0:T(8,128)}), (f32[128,1536]{1,0:T(8,128)}, f32[128,1536]{1,0:T(8,128)}, f32[128,1536]{1,0:T(8,128)}, ...) | async-done | bytes 3145744 | tf_op jit(solution)/shard_map/psum | solution.py:246
  788.2 4.1 fusion.58
  (477 shorter events, 328.5 us)
Async XLA Ops:
  6.5 682.6 %copy-start = (bf16[1024,1536]{1,0:T(8,128)(2,1)S(1)}, bf16[1024,1536]{1,0:T(8,128)(2,1)}, u32[]{:S(2)}) copy-start(bf16[1024,1536]{1,0:T(8,128)(2,1)} %param.35) | copy-start | bytes 9437188
  9.8 19.8 %all-to-all-start = ((f32[32,1,1]{2,1,0:T(1,128)}), f32[32,1,1]{2,1,0:T(1,128)S(1)}, u32[]{:S(2)}, u32[]{:S(2)}) async-start(f32[32,1,1]{2,1,0:T(1,128)} %copy.719), calls=%async_computation | async-start | bytes 32768 | tf_op jit(solution)/shard_map/all_to_all | solution.py:154
  32.6 49.4 %all-to-all-start.9 = ((bf16[32,128,1,384]{3,1,2,0:T(8,128)(2,1)}), bf16[32,128,1,384]{3,1,2,0:T(8,128)(2,1)}, u32[]{:S(2)}, u32[]{:S(2)}) async-start(bf16[32,128,1,384]{3,1,2,0:T(8,128)(2,1)} %stack.22), calls=%async_computation.9 | async-start | bytes 6291456 | tf_op jit(solution)/shard_map/all_to_all | solution.py:136
  57.2 56.0 %copy-start.54 = (f32[512,6]{0,1:T(8,128)}, f32[512,6]{0,1:T(8,128)S(1)}, u32[]{:S(2)}) copy-start(f32[512,6]{0,1:T(8,128)S(1)} %fusion.110) | copy-start | bytes 36868
  57.4 50.3 %copy-start.81 = (s32[1024]{0:T(1024)}, s32[1024]{0:T(1024)S(1)}, u32[]{:S(2)}) copy-start(s32[1024]{0:T(1024)S(1)} %pad_clamp_fusion.2) | copy-start | bytes 12292
  63.8 18.2 %copy-start.36 = (bf16[128,384]{1,0:T(8,128)(2,1)S(1)}, bf16[128,384]{1,0:T(8,128)(2,1)}, u32[]{:S(2)}) copy-start(bf16[128,384]{1,0:T(8,128)(2,1)} %get-tuple-element.86) | copy-start | bytes 294916
  84.2 47.2 %all-to-all-start.5 = ((bf16[32,128,1,384]{3,1,2,0:T(8,128)(2,1)}), bf16[32,128,1,384]{3,1,2,0:T(8,128)(2,1)}, u32[]{:S(2)}, u32[]{:S(2)}) async-start(bf16[32,128,1,384]{3,1,2,0:T(8,128)(2,1)} %stack.20), calls=%async_computation.5 | async-start | bytes 6291456 | tf_op jit(solution)/shard_map/all_to_all | solution.py:136
  134.6 95.2 %all-to-all-start.13 = ((bf16[32,128,1,384]{3,1,2,0:T(8,128)(2,1)}), bf16[32,128,1,384]{3,1,2,0:T(8,128)(2,1)}, u32[]{:S(2)}, u32[]{:S(2)}) async-start(bf16[32,128,1,384]{3,1,2,0:T(8,128)(2,1)} %stack.24), calls=%async_computation.13 | async-start | bytes 6291456 | tf_op jit(solution)/shard_map/all_to_all | solution.py:136
  151.0 22.0 %copy-start.41 = (f32[32,8,1,6]{1,2,3,0:T(1,128)S(1)}, f32[32,8,1,6]{1,2,3,0:T(1,128)}, u32[]{:S(2)}) copy-start(f32[32,8,1,6]{1,2,3,0:T(1,128)} %get-tuple-element.76) | copy-start | bytes 18436
  168.8 19.6 %copy-start.73 = (f32[128,6]{0,1:T(8,128)S(1)}, f32[128,6]{0,1:T(8,128)}, u32[]{:S(2)}) copy-start(f32[128,6]{0,1:T(8,128)} %copy.819) | copy-start | bytes 9220
  169.8 20.0 %copy-start.58 = (f32[128,6]{0,1:T(8,128)S(1)}, f32[128,6]{0,1:T(8,128)}, u32[]{:S(2)}) copy-start(f32[128,6]{0,1:T(8,128)} %slice_add_fusion.1) | copy-start | bytes 9220
  204.0 14.3 %copy-start.35 = (bf16[2,128,384]{1,2,0:T(8,128)(2,1)S(1)}, bf16[2,128,384]{1,2,0:T(8,128)(2,1)}, u32[]{:S(2)}) copy-start(bf16[2,128,384]{1,2,0:T(8,128)(2,1)} %copy.786) | copy-start | bytes 589828
  213.2 16.4 %copy-start.84 = (s32[16]{0:T(128)S(1)}, s32[16]{0:T(128)}, u32[]{:S(2)}) copy-start(s32[16]{0:T(128)} %get-tuple-element.112) | copy-start | bytes 196
  232.9 49.4 %all-to-all-start.1 = ((bf16[32,128,1,384]{3,1,2,0:T(8,128)(2,1)}), bf16[32,128,1,384]{3,1,2,0:T(8,128)(2,1)}, u32[]{:S(2)}, u32[]{:S(2)}) async-start(bf16[32,128,1,384]{3,1,2,0:T(8,128)(2,1)} %stack.18), calls=%async_computation.1 | async-start | bytes 6291456 | tf_op jit(solution)/shard_map/all_to_all | solution.py:136
  242.6 111.3 %copy-start.61 = (s32[1024]{0:T(1024)}, s32[1024]{0:T(1024)S(1)}, u32[]{:S(2)}) copy-start(s32[1024]{0:T(1024)S(1)} %pad_clamp_fusion.3) | copy-start | bytes 12292
  242.7 84.9 %copy-start.86 = (pred[32]{0:T(512)(128)(4,1)}, pred[32]{0:T(512)(128)(4,1)S(1)}, u32[]{:S(2)}) copy-start(pred[32]{0:T(512)(128)(4,1)S(1)} %fusion.115) | copy-start | bytes 100
  330.6 30.8 %all-to-all-start.2 = ((f32[32,1,8,1,6]{2,3,4,1,0:T(1,128)}), f32[32,1,8,1,6]{2,3,4,1,0:T(1,128)}, u32[]{:S(2)}, u32[]{:S(2)}) async-start(f32[32,1,8,1,6]{2,3,4,1,0:T(1,128)} %copy.728), calls=%async_computation.2 | async-start | bytes 196608 | tf_op jit(solution)/shard_map/all_to_all | solution.py:165
  349.5 21.1 %copy-start.87 = (pred[32]{0:T(512)(128)(4,1)S(1)}, pred[32]{0:T(512)(128)(4,1)}, u32[]{:S(2)}) copy-start(pred[32]{0:T(512)(128)(4,1)} %copy-done.86) | copy-start | bytes 100
  355.3 19.6 %copy-start.51 = (f32[32,1,8,1,6]{0,2,4,3,1:T(8,128)S(1)}, f32[32,1,8,1,6]{0,2,4,3,1:T(8,128)}, u32[]{:S(2)}) copy-start(f32[32,1,8,1,6]{0,2,4,3,1:T(8,128)} %get-tuple-element.110) | copy-start | bytes 18436
  355.3 20.3 %copy-start.50 = (f32[32,1,8,1,6]{0,2,4,3,1:T(8,128)S(1)}, f32[32,1,8,1,6]{0,2,4,3,1:T(8,128)}, u32[]{:S(2)}) copy-start(f32[32,1,8,1,6]{0,2,4,3,1:T(8,128)} %get-tuple-element.107) | copy-start | bytes 18436
  355.3 21.0 %copy-start.49 = (f32[32,1,8,1,6]{0,2,4,3,1:T(8,128)S(1)}, f32[32,1,8,1,6]{0,2,4,3,1:T(8,128)}, u32[]{:S(2)}) copy-start(f32[32,1,8,1,6]{0,2,4,3,1:T(8,128)} %get-tuple-element.109) | copy-start | bytes 18436
  355.3 21.7 %copy-start.48 = (f32[32,1,8,1,6]{0,2,4,3,1:T(8,128)S(1)}, f32[32,1,8,1,6]{0,2,4,3,1:T(8,128)}, u32[]{:S(2)}) copy-start(f32[32,1,8,1,6]{0,2,4,3,1:T(8,128)} %get-tuple-element.104) | copy-start | bytes 18436
  357.2 30.8 %copy-start.46 = (f32[32,8,1,6]{0,1,3,2:T(8,128)S(1)}, f32[32,8,1,6]{0,1,3,2:T(8,128)}, u32[]{:S(2)}) copy-start(f32[32,8,1,6]{0,1,3,2:T(8,128)} %copy.730) | copy-start | bytes 18436
  357.2 30.8 %copy-start.47 = (f32[32,8,1,6]{0,1,3,2:T(8,128)S(1)}, f32[32,8,1,6]{0,1,3,2:T(8,128)}, u32[]{:S(2)}) copy-start(f32[32,8,1,6]{0,1,3,2:T(8,128)} %copy.751) | copy-start | bytes 18436
  358.4 56.3 %copy-start.44 = (f32[32,8,1,6]{0,1,3,2:T(8,128)S(1)}, f32[32,8,1,6]{0,1,3,2:T(8,128)}, u32[]{:S(2)}) copy-start(f32[32,8,1,6]{0,1,3,2:T(8,128)} %copy.777) | copy-start | bytes 18436
  358.4 56.3 %copy-start.45 = (f32[32,8,1,6]{0,1,3,2:T(8,128)S(1)}, f32[32,8,1,6]{0,1,3,2:T(8,128)}, u32[]{:S(2)}) copy-start(f32[32,8,1,6]{0,1,3,2:T(8,128)} %copy.809) | copy-start | bytes 18436
  360.0 14.1 %copy-start.52 = (f32[32,1,8,1,6]{0,2,4,3,1:T(8,128)S(1)}, f32[32,1,8,1,6]{0,2,4,3,1:T(8,128)}, u32[]{:S(2)}) copy-start(f32[32,1,8,1,6]{0,2,4,3,1:T(8,128)} %get-tuple-element.108) | copy-start | bytes 18436
  361.5 18.1 %all-to-all-start.6 = ((f32[32,1,8,1,6]{2,3,4,1,0:T(1,128)}), f32[32,1,8,1,6]{2,3,4,1,0:T(1,128)S(1)}, u32[]{:S(2)}, u32[]{:S(2)}) async-start(f32[32,1,8,1,6]{2,3,4,1,0:T(1,128)} %copy.749), calls=%async_computation.6 | async-start | bytes 196608 | tf_op jit(solution)/shard_map/all_to_all | solution.py:165
  379.6 17.3 %all-to-all-start.10 = ((f32[32,1,8,1,6]{2,3,4,1,0:T(1,128)}), f32[32,1,8,1,6]{2,3,4,1,0:T(1,128)S(1)}, u32[]{:S(2)}, u32[]{:S(2)}) async-start(f32[32,1,8,1,6]{2,3,4,1,0:T(1,128)} %copy.775), calls=%async_computation.10 | async-start | bytes 196608 | tf_op jit(solution)/shard_map/all_to_all | solution.py:165
  388.2 77.4 %copy-start.37 = (f32[64,8,6]{0,1,2:T(8,128)}, f32[64,8,6]{0,1,2:T(8,128)S(1)}, u32[]{:S(2)}) copy-start(f32[64,8,6]{0,1,2:T(8,128)S(1)} %get-tuple-element.124) | copy-start | bytes 36868
  396.9 13.2 %all-to-all-start.14 = ((f32[32,1,8,1,6]{2,3,4,1,0:T(1,128)}), f32[32,1,8,1,6]{2,3,4,1,0:T(1,128)S(1)}, u32[]{:S(2)}, u32[]{:S(2)}) async-start(f32[32,1,8,1,6]{2,3,4,1,0:T(1,128)} %copy.807), calls=%async_computation.14 | async-start | bytes 196608 | tf_op jit(solution)/shard_map/all_to_all | solution.py:165
  402.0 63.6 %copy-start.30 = (f32[16,8,6]{1,2,0:T(8,128)}, f32[16,8,6]{1,2,0:T(8,128)S(1)}, u32[]{:S(2)}) copy-start(f32[16,8,6]{1,2,0:T(8,128)S(1)} %select_reduce_fusion.3) | copy-start | bytes 9220
  410.1 12.8 %all-to-all-start.4 = ((f32[32,1,8,1,6]{2,3,4,1,0:T(1,128)}), f32[32,1,8,1,6]{2,3,4,1,0:T(1,128)S(1)}, u32[]{:S(2)}, u32[]{:S(2)}) async-start(f32[32,1,8,1,6]{2,3,4,1,0:T(1,128)} %copy.741), calls=%async_computation.4 | async-start | bytes 196608 | tf_op jit(solution)/shard_map/all_to_all | solution.py:178
  415.5 50.1 %copy-start.38 = (f32[64,8,6]{0,1,2:T(8,128)}, f32[64,8,6]{0,1,2:T(8,128)S(1)}, u32[]{:S(2)}) copy-start(f32[64,8,6]{0,1,2:T(8,128)S(1)} %get-tuple-element.125) | copy-start | bytes 36868
  415.5 50.1 %copy-start.39 = (f32[64,8,6]{0,1,2:T(8,128)}, f32[64,8,6]{0,1,2:T(8,128)S(1)}, u32[]{:S(2)}) copy-start(f32[64,8,6]{0,1,2:T(8,128)S(1)} %get-tuple-element.126) | copy-start | bytes 36868
  422.9 12.7 %all-to-all-start.16 = ((f32[32,1,8,1,6]{2,3,4,1,0:T(1,128)}), f32[32,1,8,1,6]{2,3,4,1,0:T(1,128)S(1)}, u32[]{:S(2)}, u32[]{:S(2)}) async-start(f32[32,1,8,1,6]{2,3,4,1,0:T(1,128)} %copy.830), calls=%async_computation.16 | async-start | bytes 196608 | tf_op jit(solution)/shard_map/all_to_all | solution.py:178
  435.6 13.5 %all-to-all-start.8 = ((f32[32,1,8,1,6]{2,3,4,1,0:T(1,128)}), f32[32,1,8,1,6]{2,3,4,1,0:T(1,128)}, u32[]{:S(2)}, u32[]{:S(2)}) async-start(f32[32,1,8,1,6]{2,3,4,1,0:T(1,128)} %copy.767), calls=%async_computation.8 | async-start | bytes 196608 | tf_op jit(solution)/shard_map/all_to_all | solution.py:178
  442.1 23.5 %copy-start.27 = (f32[16,8,6]{1,2,0:T(8,128)}, f32[16,8,6]{1,2,0:T(8,128)S(1)}, u32[]{:S(2)}) copy-start(f32[16,8,6]{1,2,0:T(8,128)S(1)} %get-tuple-element.10) | copy-start | bytes 9220
  442.1 23.6 %copy-start.28 = (f32[16,8,6]{1,2,0:T(8,128)}, f32[16,8,6]{1,2,0:T(8,128)S(1)}, u32[]{:S(2)}) copy-start(f32[16,8,6]{1,2,0:T(8,128)S(1)} %get-tuple-element.11) | copy-start | bytes 9220
  442.1 23.6 %copy-start.29 = (f32[16,8,6]{1,2,0:T(8,128)}, f32[16,8,6]{1,2,0:T(8,128)S(1)}, u32[]{:S(2)}) copy-start(f32[16,8,6]{1,2,0:T(8,128)S(1)} %get-tuple-element.12) | copy-start | bytes 9220
  449.1 16.5 %all-to-all-start.12 = ((f32[32,1,8,1,6]{2,3,4,1,0:T(1,128)}), f32[32,1,8,1,6]{2,3,4,1,0:T(1,128)}, u32[]{:S(2)}, u32[]{:S(2)}) async-start(f32[32,1,8,1,6]{2,3,4,1,0:T(1,128)} %copy.798), calls=%async_computation.12 | async-start | bytes 196608 | tf_op jit(solution)/shard_map/all_to_all | solution.py:178
  465.6 35.7 %all-to-all-start.3 = ((f32[32,1,8,1,384]{4,2,3,1,0:T(8,128)}), f32[32,1,8,1,384]{4,2,3,1,0:T(8,128)S(1)}, u32[]{:S(2)}, u32[]{:S(2)}) async-start(f32[32,1,8,1,384]{4,2,3,1,0:T(8,128)} %get-tuple-element.103), calls=%async_computation.3 | async-start | bytes 786432 | tf_op jit(solution)/shard_map/all_to_all | solution.py:191
  501.4 22.4 %all-to-all-start.7 = ((f32[32,1,8,1,384]{4,2,3,1,0:T(8,128)}), f32[32,1,8,1,384]{4,2,3,1,0:T(8,128)}, u32[]{:S(2)}, u32[]{:S(2)}) async-start(f32[32,1,8,1,384]{4,2,3,1,0:T(8,128)} %get-tuple-element.101), calls=%async_computation.7 | async-start | bytes 786432 | tf_op jit(solution)/shard_map/all_to_all | solution.py:191
  523.8 28.9 %all-to-all-start.15 = ((f32[32,1,8,1,384]{4,2,3,1,0:T(8,128)}), f32[32,1,8,1,384]{4,2,3,1,0:T(8,128)S(1)}, u32[]{:S(2)}, u32[]{:S(2)}) async-start(f32[32,1,8,1,384]{4,2,3,1,0:T(8,128)} %get-tuple-element.102), calls=%async_computation.15 | async-start | bytes 786432 | tf_op jit(solution)/shard_map/all_to_all | solution.py:191
  552.7 24.4 %all-to-all-start.11 = ((f32[32,1,8,1,384]{4,2,3,1,0:T(8,128)}), f32[32,1,8,1,384]{4,2,3,1,0:T(8,128)}, u32[]{:S(2)}, u32[]{:S(2)}) async-start(f32[32,1,8,1,384]{4,2,3,1,0:T(8,128)} %get-tuple-element.100), calls=%async_computation.11 | async-start | bytes 786432 | tf_op jit(solution)/shard_map/all_to_all | solution.py:191
  562.1 118.6 %all-reduce.7.cloned.1.call-start = ((), (), s32[]{:S(2)}) async-start(), calls=%async_computation.18 | async-start | bytes 6291456 | tf_op jit(solution)/shard_map/psum | solution.py:240
  593.0 90.7 %copy-start.80 = (f32[1536]{0:T(1024)S(1)}, f32[1536]{0:T(1024)}, u32[]{:S(2)}) copy-start(f32[1536]{0:T(1024)} %param.32) | copy-start | bytes 18436
  593.0 195.2 %all-reduce.5.cloned.1.call-start = ((), (), s32[]{:S(2)}) async-start(), calls=%async_computation.17 | async-start | bytes 6291456 | tf_op jit(solution)/shard_map/psum | solution.py:246
  (70 other events, 443.0 us)
Sparse Core Ops, SparseCore 0:
  593.1 87.4 all-reduce.6
  712.2 75.9 all-reduce.4
